TPU v7x, 128 devices: a whole 4x4x4 slice. The times are simulated.
128 devices in a mesh: row: 8 (over y, x_hi), col: 16 (over x_lo, z, core).
Axes of the slice: x: 4 (x_hi: 2, x_lo: 2; x = x_hi * 2 + x_lo), y: 4, z: 4, core: 2. Of those that a mesh axis runs over, the one named last changes fastest.
Arguments:
- affinity: bfloat16 [8, 16, 32, 256, 256], P('row', 'col'), may hold values from 9e-05 to 32.4
- block_rows: int32 [8, 16, 32], P('row', 'col'), may hold values from 0 to 7, as said below
- block_cols: int32 [8, 16, 32], P('row', 'col'), may hold values from 0 to 15
- block_count: int32 [8, 16], P('row', 'col'), may hold values from 8 to 32, as said below
- labels: float32 [32768, 1024], P(('row', 'col')), may hold values from 0 to 1
- labelled: int32 [32768], P(('row', 'col')), may hold values 0 or 1
Outputs:
- scores: float32 [32768, 1024], P(('row', 'col'))
Inputs may be any that keep to these rules, and one draw needn't show every extreme that they name: Within one entry (r, c) the pairs (block_rows, block_cols) of all 32 slots are distinct, and its first 8 slots name every row block once. `block_count`: some entry has all 32 slots live.
All inputs are finite; a program needn't handle non-finite values. No bound on the sum of `labelled` on one device may be relied on, other than what follows from the above.
Results may differ from a plain program's by a relative error of at most 0.0003.
Values may be sent and summed in bfloat16 or wider, within the bound.
A program may use at most 128 MiB of HBM per device.

v0:
```python
import jax
import jax.numpy as jnp
from jax import lax
from jax.sharding import PartitionSpec as P

SWEEPS = 2
spread_weight = 0.8


def group_term(tile_stack, row_ids, col_ids, slot_live, gathered, group_id, group_width):
    first_slot = group_id * group_width
    tile_group = lax.dynamic_slice_in_dim(tile_stack, first_slot, group_width, 0)
    group_rows = lax.dynamic_slice_in_dim(row_ids, first_slot, group_width, 0)
    group_cols = lax.dynamic_slice_in_dim(col_ids, first_slot, group_width, 0)
    group_live = lax.dynamic_slice_in_dim(slot_live, first_slot, group_width, 0)
    fetched = jnp.take(gathered, group_cols, axis=0)
    product = jnp.einsum("gij,gjc->gic", tile_group, fetched, preferred_element_type=jnp.float32)
    placing = (
        (group_rows[None, :] == jnp.arange(group_width)[:, None]) & group_live[None, :]
    ).astype(jnp.float32)
    return jnp.einsum("rg,gic->ric", placing, product, precision=lax.Precision.HIGHEST)


def on_device(affinity, block_rows, block_cols, block_count, labels, labelled):
    tile_stack = affinity[0, 0]
    row_ids = block_rows[0, 0]
    col_ids = block_cols[0, 0]
    live_count = block_count[0, 0]
    row_groups = lax.axis_size("row")
    col_groups = lax.axis_size("col")
    slot_total = tile_stack.shape[0]
    tile_rows = tile_stack.shape[1]
    classes = labels.shape[1]
    slot_live = jnp.arange(slot_total) < live_count
    placing = ((row_ids[None, :] == jnp.arange(row_groups)[:, None]) & slot_live[None, :]).astype(
        jnp.float32
    )
    row_sums = jnp.sum(tile_stack, axis=2, dtype=jnp.float32)
    degree_part = jnp.dot(placing, row_sums, precision=lax.Precision.HIGHEST)
    degree = lax.psum_scatter(degree_part, "row", scatter_dimension=0, tiled=True).reshape(
        tile_rows, 1
    )
    keep_rows = labelled[:, None] == 1
    current = labels
    group_total = slot_total // row_groups
    for iteration in range(SWEEPS):
        gathered = lax.all_gather(current.astype(jnp.bfloat16), "col", axis=0, tiled=True)
        gathered = gathered.reshape(col_groups, tile_rows, classes)

        def add_group(group_id, running):
            return running + group_term(
                tile_stack, row_ids, col_ids, slot_live, gathered, group_id, row_groups
            )

        empty = jnp.zeros((row_groups, tile_rows, classes), jnp.float32)
        running = lax.fori_loop(0, group_total, add_group, empty)
        flat_terms = running.reshape(row_groups * tile_rows, classes)
        summed = lax.psum_scatter(flat_terms, "row", scatter_dimension=0, tiled=True)
        spread = spread_weight * summed / degree + (1.0 - spread_weight) * labels
        current = jnp.where(keep_rows, labels, spread)
    return current


def solution(mesh):
    placed = (
        P("row", "col", None, None, None),
        P("row", "col", None),
        P("row", "col", None),
        P("row", "col"),
        P(("row", "col"), None),
        P(("row", "col")),
    )
    return jax.shard_map(
        on_device, mesh=mesh, in_specs=placed, out_specs=P(("row", "col"), None), check_vma=False
    )
```

profile of v0, /device:TPU:1, one launch (start us, length us, event | category | flops | bytes accessed | tf_op | source)
XLA Modules:
  0.0 628.7 jit_solution(13757299641391947367)
XLA Ops:
  9.4 55.5 %all-gather.3.cloned.1.call-done = bf16[4096,1024]{1,0:T(8,128)(2,1)} async-done(((bf16[256,1024]{1,0:T(8,128)(2,1)}), bf16[4096,1024]{1,0:T(8,128)(2,1)}) %all-gather.3.cloned.1.call-update) | async-done | bytes 8388624 | tf_op jit(solution)/shard_map/all_gather | solution.py:47
  64.9 125.6 %while.28 = (s32[]{:T(128)}, f32[8,256,1024]{2,0,1:T(8,128)}, s32[32]{0:T(128)}, pred[32]{0:T(512)(128)(4,1)S(1)}, bf16[32,256,256]{2,1,0:T(8,128)(2,1)}, /*inde...) while((s32[]{:T(128)}, f32[8,256,1024]{2,0,1:T(8,128)}, ...), condition=%wide.region_1.3_spmd.clone, body=%wide.region_0.2_spmd.clone.sunk | while | flops 1281361024 | bytes 47191000 | solution.py:56
  65.6 6.2 gather_fusion
  71.8 7.1 %fusion.52 = f32[8,256,1024]{2,1,0:T(8,128)} fusion(bf16[8,256,1024]{2,1,0:T(8,128)(2,1)} %gather_fusion, pred[8]{0:T(512)(128)(4,1)S(1)} %get-tuple-element.420, bf16[32,256,256]{2,1,0:T(8,128)(2,1)} %get-tuple-element.456, s32[]{:T(128)S(6)} %select_n.59), kind=kOutput, calls=%fused_computation.5.clone.1 | convolution fusion | flops 1075838976 | bytes 13631500 | tf_op jit(solution)/shard_map/while/body/eval_jaxpr/gij,gjc->gic/dot_general | solution.py:17
  79.0 15.5 %select_add_fusion.4 = f32[8,256,1024]{2,0,1:T(8,128)} fusion(f32[8,256,1024]{2,0,1:T(8,128)} %get-tuple-element.442, pred[]{:T(512)S(6)} %compare.6, f32[8,256,1024]{2,1,0:T(8,128)} %fusion.52, s32[8]{0:T(128)S(1)} %dynamic_slice.79, pred[8]{0:T(512)(128)(4,1)S(1)} %dynamic_slice.80), kind=kOutput, calls=%fused_computation.4.clone.1 | convolution fusion | flops 205521024 | bytes 25165864 | tf_op jit(solution)/shard_map/while/body/eval_jaxpr/rg,gic->ric/dot_general | solution.py:21
  95.2 6.2 gather_fusion
  101.4 7.1 %fusion.52 = f32[8,256,1024]{2,1,0:T(8,128)} fusion(bf16[8,256,1024]{2,1,0:T(8,128)(2,1)} %gather_fusion, pred[8]{0:T(512)(128)(4,1)S(1)} %get-tuple-element.420, bf16[32,256,256]{2,1,0:T(8,128)(2,1)} %get-tuple-element.456, s32[]{:T(128)S(6)} %select_n.59), kind=kOutput, calls=%fused_computation.5.clone.1 | convolution fusion | flops 1075838976 | bytes 13631500 | tf_op jit(solution)/shard_map/while/body/eval_jaxpr/gij,gjc->gic/dot_general | solution.py:17
  108.6 17.9 %select_add_fusion.4 = f32[8,256,1024]{2,0,1:T(8,128)} fusion(f32[8,256,1024]{2,0,1:T(8,128)} %get-tuple-element.442, pred[]{:T(512)S(6)} %compare.6, f32[8,256,1024]{2,1,0:T(8,128)} %fusion.52, s32[8]{0:T(128)S(1)} %dynamic_slice.79, pred[8]{0:T(512)(128)(4,1)S(1)} %dynamic_slice.80), kind=kOutput, calls=%fused_computation.4.clone.1 | convolution fusion | flops 205521024 | bytes 25165864 | tf_op jit(solution)/shard_map/while/body/eval_jaxpr/rg,gic->ric/dot_general | solution.py:21
  127.2 6.2 gather_fusion
  133.4 7.1 %fusion.52 = f32[8,256,1024]{2,1,0:T(8,128)} fusion(bf16[8,256,1024]{2,1,0:T(8,128)(2,1)} %gather_fusion, pred[8]{0:T(512)(128)(4,1)S(1)} %get-tuple-element.420, bf16[32,256,256]{2,1,0:T(8,128)(2,1)} %get-tuple-element.456, s32[]{:T(128)S(6)} %select_n.59), kind=kOutput, calls=%fused_computation.5.clone.1 | convolution fusion | flops 1075838976 | bytes 13631500 | tf_op jit(solution)/shard_map/while/body/eval_jaxpr/gij,gjc->gic/dot_general | solution.py:17
  140.6 17.9 %select_add_fusion.4 = f32[8,256,1024]{2,0,1:T(8,128)} fusion(f32[8,256,1024]{2,0,1:T(8,128)} %get-tuple-element.442, pred[]{:T(512)S(6)} %compare.6, f32[8,256,1024]{2,1,0:T(8,128)} %fusion.52, s32[8]{0:T(128)S(1)} %dynamic_slice.79, pred[8]{0:T(512)(128)(4,1)S(1)} %dynamic_slice.80), kind=kOutput, calls=%fused_computation.4.clone.1 | convolution fusion | flops 205521024 | bytes 25165864 | tf_op jit(solution)/shard_map/while/body/eval_jaxpr/rg,gic->ric/dot_general | solution.py:21
  159.2 6.2 gather_fusion
  165.4 7.1 %fusion.52 = f32[8,256,1024]{2,1,0:T(8,128)} fusion(bf16[8,256,1024]{2,1,0:T(8,128)(2,1)} %gather_fusion, pred[8]{0:T(512)(128)(4,1)S(1)} %get-tuple-element.420, bf16[32,256,256]{2,1,0:T(8,128)(2,1)} %get-tuple-element.456, s32[]{:T(128)S(6)} %select_n.59), kind=kOutput, calls=%fused_computation.5.clone.1 | convolution fusion | flops 1075838976 | bytes 13631500 | tf_op jit(solution)/shard_map/while/body/eval_jaxpr/gij,gjc->gic/dot_general | solution.py:17
  172.6 17.9 %select_add_fusion.4 = f32[8,256,1024]{2,0,1:T(8,128)} fusion(f32[8,256,1024]{2,0,1:T(8,128)} %get-tuple-element.442, pred[]{:T(512)S(6)} %compare.6, f32[8,256,1024]{2,1,0:T(8,128)} %fusion.52, s32[8]{0:T(128)S(1)} %dynamic_slice.79, pred[8]{0:T(512)(128)(4,1)S(1)} %dynamic_slice.80), kind=kOutput, calls=%fused_computation.4.clone.1 | convolution fusion | flops 205521024 | bytes 25165864 | tf_op jit(solution)/shard_map/while/body/eval_jaxpr/rg,gic->ric/dot_general | solution.py:21
  190.5 11.5 %copy.9 = f32[8,256,1024]{2,1,0:T(8,128)} copy(f32[8,256,1024]{2,0,1:T(8,128)} %get-tuple-element.254) | data formatting | bytes 16777216 | tf_op jit(solution)/shard_map/while | solution.py:56
  206.6 21.5 %all-reduce = f32[8,256]{1,0:T(8,128)S(1)} all-reduce(f32[8,256]{1,0:T(8,128)S(1)} %fusion.33), channel_id=3, replica_groups=mesh['row'=8,'col'=16] {'row'}, use_global_device_ids=true, to_apply=%region_4.6.clone | all-reduce | flops 2048 | bytes 16384
  228.8 88.5 %reduce-scatter.3.cloned.1.call-done = f32[256,1024]{1,0:T(8,128)} async-done(((f32[2048,1024]{1,0:T(8,128)}), f32[256,1024]{1,0:T(8,128)}) %reduce-scatter.3.cloned.1.call-update) | async-done | bytes 1048592 | tf_op jit(solution)/shard_map/reduce_scatter | solution.py:58
  319.8 51.2 %all-gather.5.cloned.1.call-done = bf16[4096,1024]{1,0:T(8,128)(2,1)} async-done(((bf16[256,1024]{1,0:T(8,128)(2,1)}), bf16[4096,1024]{1,0:T(8,128)(2,1)}) %all-gather.5.cloned.1.call-update) | async-done | bytes 8388624 | tf_op jit(solution)/shard_map/all_gather | solution.py:47
  371.0 122.9 %while.29 = (s32[]{:T(128)}, f32[8,256,1024]{2,0,1:T(8,128)}, s32[32]{0:T(128)S(1)}, pred[32]{0:T(512)(128)(4,1)S(1)}, bf16[32,256,256]{2,1,0:T(8,128)(2,1)}, /*...) while((s32[]{:T(128)}, f32[8,256,1024]{2,0,1:T(8,128)}, ...), condition=%wide.region_6.8_spmd.clone, body=%wide.region_5.7_spmd.clone.sunk | while | flops 1281361024 | bytes 47190460 | solution.py:56
  371.1 6.2 gather_fusion.1
  377.2 7.1 %fusion.57 = f32[8,256,1024]{2,1,0:T(8,128)} fusion(bf16[8,256,1024]{2,1,0:T(8,128)(2,1)} %gather_fusion.1, pred[8]{0:T(512)(128)(4,1)S(1)} %get-tuple-element.429, bf16[32,256,256]{2,1,0:T(8,128)(2,1)} %get-tuple-element.489, s32[]{:T(128)S(6)} %select_n.61), kind=kOutput, calls=%fused_computation.23.clone.1 | convolution fusion | flops 1075838976 | bytes 13631500 | tf_op jit(solution)/shard_map/while/body/eval_jaxpr/gij,gjc->gic/dot_general | solution.py:17
  384.5 15.4 %select_add_fusion.5 = f32[8,256,1024]{2,0,1:T(8,128)} fusion(f32[8,256,1024]{2,0,1:T(8,128)} %get-tuple-element.475, pred[]{:T(512)S(6)} %compare.7, f32[8,256,1024]{2,1,0:T(8,128)} %fusion.57, s32[8]{0:T(128)S(1)} %dynamic_slice.82, pred[8]{0:T(512)(128)(4,1)S(1)} %dynamic_slice.83), kind=kOutput, calls=%fused_computation.22.clone.1 | convolution fusion | flops 205521024 | bytes 25165864 | tf_op jit(solution)/shard_map/while/body/eval_jaxpr/rg,gic->ric/dot_general | solution.py:21
  400.0 6.2 gather_fusion.1
  406.2 7.1 %fusion.57 = f32[8,256,1024]{2,1,0:T(8,128)} fusion(bf16[8,256,1024]{2,1,0:T(8,128)(2,1)} %gather_fusion.1, pred[8]{0:T(512)(128)(4,1)S(1)} %get-tuple-element.429, bf16[32,256,256]{2,1,0:T(8,128)(2,1)} %get-tuple-element.489, s32[]{:T(128)S(6)} %select_n.61), kind=kOutput, calls=%fused_computation.23.clone.1 | convolution fusion | flops 1075838976 | bytes 13631500 | tf_op jit(solution)/shard_map/while/body/eval_jaxpr/gij,gjc->gic/dot_general | solution.py:17
  413.4 17.8 %select_add_fusion.5 = f32[8,256,1024]{2,0,1:T(8,128)} fusion(f32[8,256,1024]{2,0,1:T(8,128)} %get-tuple-element.475, pred[]{:T(512)S(6)} %compare.7, f32[8,256,1024]{2,1,0:T(8,128)} %fusion.57, s32[8]{0:T(128)S(1)} %dynamic_slice.82, pred[8]{0:T(512)(128)(4,1)S(1)} %dynamic_slice.83), kind=kOutput, calls=%fused_computation.22.clone.1 | convolution fusion | flops 205521024 | bytes 25165864 | tf_op jit(solution)/shard_map/while/body/eval_jaxpr/rg,gic->ric/dot_general | solution.py:21
  431.3 6.2 gather_fusion.1
  437.5 7.1 %fusion.57 = f32[8,256,1024]{2,1,0:T(8,128)} fusion(bf16[8,256,1024]{2,1,0:T(8,128)(2,1)} %gather_fusion.1, pred[8]{0:T(512)(128)(4,1)S(1)} %get-tuple-element.429, bf16[32,256,256]{2,1,0:T(8,128)(2,1)} %get-tuple-element.489, s32[]{:T(128)S(6)} %select_n.61), kind=kOutput, calls=%fused_computation.23.clone.1 | convolution fusion | flops 1075838976 | bytes 13631500 | tf_op jit(solution)/shard_map/while/body/eval_jaxpr/gij,gjc->gic/dot_general | solution.py:17
  444.7 17.8 %select_add_fusion.5 = f32[8,256,1024]{2,0,1:T(8,128)} fusion(f32[8,256,1024]{2,0,1:T(8,128)} %get-tuple-element.475, pred[]{:T(512)S(6)} %compare.7, f32[8,256,1024]{2,1,0:T(8,128)} %fusion.57, s32[8]{0:T(128)S(1)} %dynamic_slice.82, pred[8]{0:T(512)(128)(4,1)S(1)} %dynamic_slice.83), kind=kOutput, calls=%fused_computation.22.clone.1 | convolution fusion | flops 205521024 | bytes 25165864 | tf_op jit(solution)/shard_map/while/body/eval_jaxpr/rg,gic->ric/dot_general | solution.py:21
  468.8 7.1 %fusion.57 = f32[8,256,1024]{2,1,0:T(8,128)} fusion(bf16[8,256,1024]{2,1,0:T(8,128)(2,1)} %gather_fusion.1, pred[8]{0:T(512)(128)(4,1)S(1)} %get-tuple-element.429, bf16[32,256,256]{2,1,0:T(8,128)(2,1)} %get-tuple-element.489, s32[]{:T(128)S(6)} %select_n.61), kind=kOutput, calls=%fused_computation.23.clone.1 | convolution fusion | flops 1075838976 | bytes 13631500 | tf_op jit(solution)/shard_map/while/body/eval_jaxpr/gij,gjc->gic/dot_general | solution.py:17
  476.0 17.8 %select_add_fusion.5 = f32[8,256,1024]{2,0,1:T(8,128)} fusion(f32[8,256,1024]{2,0,1:T(8,128)} %get-tuple-element.475, pred[]{:T(512)S(6)} %compare.7, f32[8,256,1024]{2,1,0:T(8,128)} %fusion.57, s32[8]{0:T(128)S(1)} %dynamic_slice.82, pred[8]{0:T(512)(128)(4,1)S(1)} %dynamic_slice.83), kind=kOutput, calls=%fused_computation.22.clone.1 | convolution fusion | flops 205521024 | bytes 25165864 | tf_op jit(solution)/shard_map/while/body/eval_jaxpr/rg,gic->ric/dot_general | solution.py:21
  493.9 11.5 %copy.10 = f32[8,256,1024]{2,1,0:T(8,128)} copy(f32[8,256,1024]{2,0,1:T(8,128)} %get-tuple-element.255) | data formatting | bytes 16777216 | tf_op jit(solution)/shard_map/while | solution.py:56
  505.4 114.3 %reduce-scatter.5.cloned.1.call-done = f32[256,1024]{1,0:T(8,128)} async-done(((f32[2048,1024]{1,0:T(8,128)}), f32[256,1024]{1,0:T(8,128)}) %reduce-scatter.5.cloned.1.call-update) | async-done | bytes 1048592 | tf_op jit(solution)/shard_map/reduce_scatter | solution.py:58
  (70 shorter events, 23.1 us)
Async XLA Ops:
  6.5 58.4 %all-gather.3.cloned.1.call-start = ((), (), s32[]{:S(2)}) async-start(), calls=%async_computation.2 | async-start | bytes 8912896 | tf_op jit(solution)/shard_map/all_gather | solution.py:47
  8.7 308.7 %reduce-scatter.3.cloned.1.call-start = ((), (), s32[]{:S(2)}) async-start(), calls=%async_computation.3 | async-start | bytes 9437184 | tf_op jit(solution)/shard_map/reduce_scatter | solution.py:58
  71.8 7.1 %copy-start.2 = (s32[32]{0:T(128)S(1)}, s32[32]{0:T(128)}, u32[]{:S(2)}) copy-start(s32[32]{0:T(128)} %get-tuple-element.454) | copy-start | bytes 388 | tf_op jit(solution)/shard_map/while
  101.4 7.1 %copy-start.2 = (s32[32]{0:T(128)S(1)}, s32[32]{0:T(128)}, u32[]{:S(2)}) copy-start(s32[32]{0:T(128)} %get-tuple-element.454) | copy-start | bytes 388 | tf_op jit(solution)/shard_map/while
  133.4 7.1 %copy-start.2 = (s32[32]{0:T(128)S(1)}, s32[32]{0:T(128)}, u32[]{:S(2)}) copy-start(s32[32]{0:T(128)} %get-tuple-element.454) | copy-start | bytes 388 | tf_op jit(solution)/shard_map/while
  165.4 7.1 %copy-start.2 = (s32[32]{0:T(128)S(1)}, s32[32]{0:T(128)}, u32[]{:S(2)}) copy-start(s32[32]{0:T(128)} %get-tuple-element.454) | copy-start | bytes 388 | tf_op jit(solution)/shard_map/while
  201.9 0.7 copy-start.5
  201.9 4.6 copy-start.3
  201.9 26.9 %copy-start.4 = (s32[256]{0:T(256)S(1)}, s32[256]{0:T(256)}, u32[]{:S(2)}) copy-start(s32[256]{0:T(256)} %param.17) | copy-start | bytes 3076
  201.9 115.5 %copy-start = (f32[256,1024]{1,0:T(8,128)S(1)}, f32[256,1024]{1,0:T(8,128)}, u32[]{:S(2)}) copy-start(f32[256,1024]{1,0:T(8,128)} %param.16) | copy-start | bytes 3145732
  201.9 169.1 %copy-start.1 = (s32[32]{0:T(128)S(1)}, s32[32]{0:T(128)}, u32[]{:S(2)}) copy-start(s32[32]{0:T(128)} %get-tuple-element.513) | copy-start | bytes 388
  202.0 169.0 %all-gather.5.cloned.1.call-start = ((), (), s32[]{:S(2)}) async-start(), calls=%async_computation.4 | async-start | bytes 8912896 | tf_op jit(solution)/shard_map/all_gather | solution.py:47
  319.7 299.9 %reduce-scatter.5.cloned.1.call-start = ((), (), s32[]{:S(2)}) async-start(), calls=%async_computation.5 | async-start | bytes 9437184 | tf_op jit(solution)/shard_map/reduce_scatter | solution.py:58
Sparse Core Ops, SparseCore 0:
  9.1 55.7 all-gather.2
  202.1 115.2 reduce-scatter.2
  319.9 51.0 all-gather.4
  505.5 114.0 reduce-scatter.4
where the time goes:
time: 630 us; the launch traced here: 629 us
  waiting for transfers between devices  310 us (49%)
  matrix products  195 us (31%)
  local copies, waits for them, and re-layouts  75.3 us (12%)
  blocking collectives  21.5 us (3%)
  between operations  13.9 us (2%)
  other arithmetic  13.6 us (2%)
    reduce_scatter x2, waiting for transfers between devices, on_device(): lax.psum_scatter(flat_terms, 'row', scatter_dimension=0, tiled=True)  203 us
    dot_general x8, matrix products, group_term(): jnp.einsum('rg,gic->ric', placing, product, precision=lax.Precision.HIGHEST)  138 us
    all_gather x2, waiting for transfers between devices, on_device(): lax.all_gather(current.astype(jnp.bfloat16), 'col', axis=0, tiled=True)  107 us
    dot_general x8, matrix products, group_term(): jnp.einsum('gij,gjc->gic', tile_group, fetched, preferred_element_type=jn...  56.6 us
    gather x8, local copies, waits for them, and re-layouts, group_term(): fetched = jnp.take(gathered, group_cols, axis=0)  49.3 us
    while x2, local copies, waits for them, and re-layouts, on_device(): running = lax.fori_loop(0, group_total, add_group, empty)  22.9 us
    unnamed x1, blocking collectives  21.5 us
  transfers between devices with their start and end apart: 4, of which 4 were waited for; matrix products, arithmetic and copies ran while one was open for 1% of the time, Pallas kernels for 0%

commit v1 on v0

--- a/solution.py
+++ b/solution.py
@@ -44,7 +44,12 @@
     current = labels
     group_total = slot_total // row_groups
     for iteration in range(SWEEPS):
-        gathered = lax.all_gather(current.astype(jnp.bfloat16), "col", axis=0, tiled=True)
+        gathered = jnp.concatenate(
+            lax.all_to_all(
+                jnp.stack([current.astype(jnp.bfloat16)] * lax.axis_size("col")), "col", 0, 0
+            ),
+            axis=0,
+        )
         gathered = gathered.reshape(col_groups, tile_rows, classes)
 
         def add_group(group_id, running):

time: 630 us -> 805 us (1.28); the launches traced: 629 us -> 796 us
  waiting for transfers between devices: 310 us -> 457 us
  starting transfers between devices: 0.13 us -> 13.7 us
  local copies, waits for them, and re-layouts: 75.3 us -> 84 us
    all_to_all x0 -> x2, waiting for transfers between devices: none -> 242 us  [on_device(): lax.all_to_all(jnp.stack([current.astype(jnp.bfloat16)] * lax.axis_size('...]
    all_gather x2 -> x0, waiting for transfers between devices: 107 us -> none  [on_device(): lax.all_gather(current.astype(jnp.bfloat16), 'col', axis=0, tiled=True)]
    all_to_all x0 -> x2, starting transfers between devices: none -> 13.6 us  [on_device(): lax.all_to_all(jnp.stack([current.astype(jnp.bfloat16)] * lax.axis_size('...]
    reduce_scatter x2, waiting for transfers between devices: 203 us -> 215 us  [on_device(): lax.psum_scatter(flat_terms, 'row', scatter_dimension=0, tiled=True)]
    another operation x0 -> x2, local copies, waits for them, and re-layouts: none -> 8.66 us  [on_device(): jnp.stack([current.astype(jnp.bfloat16)] * lax.axis_size('col'))]
where the time goes in v1:
time: 805 us; the launch traced here: 796 us
  waiting for transfers between devices  457 us (57%)
  matrix products  195 us (24%)
  local copies, waits for them, and re-layouts  84 us (10%)
  blocking collectives  21.3 us (3%)
  between operations  14.4 us (2%)
  starting transfers between devices  13.7 us (2%)
  other arithmetic  9.39 us (1%)
    all_to_all x2, waiting for transfers between devices, on_device(): lax.all_to_all(jnp.stack([current.astype(jnp.bfloat16)] * lax.axis_size('...  242 us
    reduce_scatter x2, waiting for transfers between devices, on_device(): lax.psum_scatter(flat_terms, 'row', scatter_dimension=0, tiled=True)  215 us
    dot_general x8, matrix products, group_term(): jnp.einsum('rg,gic->ric', placing, product, precision=lax.Precision.HIGHEST)  138 us
    dot_general x8, matrix products, group_term(): jnp.einsum('gij,gjc->gic', tile_group, fetched, preferred_element_type=jn...  56.6 us
    gather x8, local copies, waits for them, and re-layouts, group_term(): fetched = jnp.take(gathered, group_cols, axis=0)  49.3 us
    while x2, local copies, waits for them, and re-layouts, on_device(): running = lax.fori_loop(0, group_total, add_group, empty)  22.9 us
    unnamed x1, blocking collectives  21.3 us
  transfers between devices with their start and end apart: 4, of which 4 were waited for; matrix products, arithmetic and copies ran while one was open for 1% of the time, Pallas kernels for 0%

profile of v1, /device:TPU:1, one launch (start us, length us, event | category | flops | bytes accessed | tf_op | source)
XLA Modules:
  0.0 795.6 jit_solution(12558515908850310680)
XLA Ops:
  12.2 7.9 all-to-all-start
  20.8 121.5 %all-to-all-done = bf16[16,256,1024]{2,1,0:T(8,128)(2,1)} async-done(((bf16[16,256,1024]{2,1,0:T(8,128)(2,1)}), bf16[16,256,1024]{2,1,0:T(8,128)(2,1)}, u32[]{:S(2)}, u32[]{:S(2)}) %all-to-all-start) | async-done | bytes 8388640 | tf_op jit(solution)/shard_map/all_to_all | solution.py:48
  142.3 123.3 %while.28 = (s32[]{:T(128)}, f32[8,256,1024]{2,0,1:T(8,128)}, s32[32]{0:T(128)S(1)}, pred[32]{0:T(512)(128)(4,1)S(1)}, bf16[32,256,256]{2,1,0:T(8,128)(2,1)}, /*...) while((s32[]{:T(128)}, f32[8,256,1024]{2,0,1:T(8,128)}, ...), condition=%wide.region_1.3_spmd.clone, body=%wide.region_0.2_spmd.clone.sunk | while | flops 1281361024 | bytes 47190460 | solution.py:61
  142.4 6.2 gather_fusion
  148.6 7.1 fusion.52
  155.8 15.4 %select_add_fusion.4 = f32[8,256,1024]{2,0,1:T(8,128)} fusion(f32[8,256,1024]{2,0,1:T(8,128)} %get-tuple-element.442, pred[]{:T(512)S(6)} %compare.6, f32[8,256,1024]{2,1,0:T(8,128)} %fusion.52, s32[8]{0:T(128)S(1)} %dynamic_slice.79, pred[8]{0:T(512)(128)(4,1)S(1)} %dynamic_slice.80), kind=kOutput, calls=%fused_computation.4.clone.1 | convolution fusion | flops 205521024 | bytes 25165864 | tf_op jit(solution)/shard_map/while/body/eval_jaxpr/rg,gic->ric/dot_general | solution.py:21
  171.3 6.2 gather_fusion
  177.5 7.1 fusion.52
  184.7 17.8 %select_add_fusion.4 = f32[8,256,1024]{2,0,1:T(8,128)} fusion(f32[8,256,1024]{2,0,1:T(8,128)} %get-tuple-element.442, pred[]{:T(512)S(6)} %compare.6, f32[8,256,1024]{2,1,0:T(8,128)} %fusion.52, s32[8]{0:T(128)S(1)} %dynamic_slice.79, pred[8]{0:T(512)(128)(4,1)S(1)} %dynamic_slice.80), kind=kOutput, calls=%fused_computation.4.clone.1 | convolution fusion | flops 205521024 | bytes 25165864 | tf_op jit(solution)/shard_map/while/body/eval_jaxpr/rg,gic->ric/dot_general | solution.py:21
  208.8 7.1 fusion.52
  216.0 17.8 %select_add_fusion.4 = f32[8,256,1024]{2,0,1:T(8,128)} fusion(f32[8,256,1024]{2,0,1:T(8,128)} %get-tuple-element.442, pred[]{:T(512)S(6)} %compare.6, f32[8,256,1024]{2,1,0:T(8,128)} %fusion.52, s32[8]{0:T(128)S(1)} %dynamic_slice.79, pred[8]{0:T(512)(128)(4,1)S(1)} %dynamic_slice.80), kind=kOutput, calls=%fused_computation.4.clone.1 | convolution fusion | flops 205521024 | bytes 25165864 | tf_op jit(solution)/shard_map/while/body/eval_jaxpr/rg,gic->ric/dot_general | solution.py:21
  234.0 6.2 gather_fusion
  240.1 7.1 fusion.52
  247.3 17.8 %select_add_fusion.4 = f32[8,256,1024]{2,0,1:T(8,128)} fusion(f32[8,256,1024]{2,0,1:T(8,128)} %get-tuple-element.442, pred[]{:T(512)S(6)} %compare.6, f32[8,256,1024]{2,1,0:T(8,128)} %fusion.52, s32[8]{0:T(128)S(1)} %dynamic_slice.79, pred[8]{0:T(512)(128)(4,1)S(1)} %dynamic_slice.80), kind=kOutput, calls=%fused_computation.4.clone.1 | convolution fusion | flops 205521024 | bytes 25165864 | tf_op jit(solution)/shard_map/while/body/eval_jaxpr/rg,gic->ric/dot_general | solution.py:21
  265.6 11.5 %copy.9 = f32[8,256,1024]{2,1,0:T(8,128)} copy(f32[8,256,1024]{2,0,1:T(8,128)} %get-tuple-element.254) | data formatting | bytes 16777216 | tf_op jit(solution)/shard_map/while | solution.py:61
  281.8 21.3 %all-reduce = f32[8,256]{1,0:T(8,128)S(1)} all-reduce(f32[8,256]{1,0:T(8,128)S(1)} %fusion.33), channel_id=3, replica_groups=mesh['row'=8,'col'=16] {'row'}, use_global_device_ids=true, to_apply=%region_4.6.clone | all-reduce | flops 2048 | bytes 16384
  303.8 95.5 %reduce-scatter.3.cloned.1.call-done = f32[256,1024]{1,0:T(8,128)} async-done(((f32[2048,1024]{1,0:T(8,128)}), f32[256,1024]{1,0:T(8,128)}) %reduce-scatter.3.cloned.1.call-update) | async-done | bytes 1048592 | tf_op jit(solution)/shard_map/reduce_scatter | solution.py:63
  411.0 120.8 %all-to-all-done.1 = bf16[16,256,1024]{2,1,0:T(8,128)(2,1)} async-done(((bf16[16,256,1024]{2,1,0:T(8,128)(2,1)}), bf16[16,256,1024]{2,1,0:T(8,128)(2,1)}, u32[]{:S(2)}, u32[]{:S(2)}) %all-to-all-start.1) | async-done | bytes 8388640 | tf_op jit(solution)/shard_map/all_to_all | solution.py:48
  531.8 123.2 %while.29 = (s32[]{:T(128)}, f32[8,256,1024]{2,0,1:T(8,128)}, s32[32]{0:T(128)S(1)}, pred[32]{0:T(512)(128)(4,1)S(1)}, bf16[32,256,256]{2,1,0:T(8,128)(2,1)}, /*...) while((s32[]{:T(128)}, f32[8,256,1024]{2,0,1:T(8,128)}, ...), condition=%wide.region_6.8_spmd.clone, body=%wide.region_5.7_spmd.clone.sunk | while | flops 1281361024 | bytes 47190460 | solution.py:61
  532.0 6.2 gather_fusion.1
  538.2 7.1 fusion.57
  545.4 15.5 %select_add_fusion.5 = f32[8,256,1024]{2,0,1:T(8,128)} fusion(f32[8,256,1024]{2,0,1:T(8,128)} %get-tuple-element.475, pred[]{:T(512)S(6)} %compare.7, f32[8,256,1024]{2,1,0:T(8,128)} %fusion.57, s32[8]{0:T(128)S(1)} %dynamic_slice.82, pred[8]{0:T(512)(128)(4,1)S(1)} %dynamic_slice.83), kind=kOutput, calls=%fused_computation.22.clone.1 | convolution fusion | flops 205521024 | bytes 25165864 | tf_op jit(solution)/shard_map/while/body/eval_jaxpr/rg,gic->ric/dot_general | solution.py:21
  561.0 6.2 gather_fusion.1
  567.1 7.1 fusion.57
  574.3 17.8 %select_add_fusion.5 = f32[8,256,1024]{2,0,1:T(8,128)} fusion(f32[8,256,1024]{2,0,1:T(8,128)} %get-tuple-element.475, pred[]{:T(512)S(6)} %compare.7, f32[8,256,1024]{2,1,0:T(8,128)} %fusion.57, s32[8]{0:T(128)S(1)} %dynamic_slice.82, pred[8]{0:T(512)(128)(4,1)S(1)} %dynamic_slice.83), kind=kOutput, calls=%fused_computation.22.clone.1 | convolution fusion | flops 205521024 | bytes 25165864 | tf_op jit(solution)/shard_map/while/body/eval_jaxpr/rg,gic->ric/dot_general | solution.py:21
  592.3 6.2 gather_fusion.1
  598.4 7.1 fusion.57
  605.7 17.8 %select_add_fusion.5 = f32[8,256,1024]{2,0,1:T(8,128)} fusion(f32[8,256,1024]{2,0,1:T(8,128)} %get-tuple-element.475, pred[]{:T(512)S(6)} %compare.7, f32[8,256,1024]{2,1,0:T(8,128)} %fusion.57, s32[8]{0:T(128)S(1)} %dynamic_slice.82, pred[8]{0:T(512)(128)(4,1)S(1)} %dynamic_slice.83), kind=kOutput, calls=%fused_computation.22.clone.1 | convolution fusion | flops 205521024 | bytes 25165864 | tf_op jit(solution)/shard_map/while/body/eval_jaxpr/rg,gic->ric/dot_general | solution.py:21
  629.8 7.1 fusion.57
  637.0 17.8 %select_add_fusion.5 = f32[8,256,1024]{2,0,1:T(8,128)} fusion(f32[8,256,1024]{2,0,1:T(8,128)} %get-tuple-element.475, pred[]{:T(512)S(6)} %compare.7, f32[8,256,1024]{2,1,0:T(8,128)} %fusion.57, s32[8]{0:T(128)S(1)} %dynamic_slice.82, pred[8]{0:T(512)(128)(4,1)S(1)} %dynamic_slice.83), kind=kOutput, calls=%fused_computation.22.clone.1 | convolution fusion | flops 205521024 | bytes 25165864 | tf_op jit(solution)/shard_map/while/body/eval_jaxpr/rg,gic->ric/dot_general | solution.py:21
  655.0 11.5 %copy.10 = f32[8,256,1024]{2,1,0:T(8,128)} copy(f32[8,256,1024]{2,0,1:T(8,128)} %get-tuple-element.255) | data formatting | bytes 16777216 | tf_op jit(solution)/shard_map/while | solution.py:61
  666.5 119.5 %reduce-scatter.5.cloned.1.call-done = f32[256,1024]{1,0:T(8,128)} async-done(((f32[2048,1024]{1,0:T(8,128)}), f32[256,1024]{1,0:T(8,128)}) %reduce-scatter.5.cloned.1.call-update) | async-done | bytes 1048592 | tf_op jit(solution)/shard_map/reduce_scatter | solution.py:63
  (62 shorter events, 39.4 us)
Async XLA Ops:
  12.2 130.1 %copy-start.1 = (s32[1,1,32]{2,1,0:T(1,128)S(1)}, s32[1,1,32]{2,1,0:T(1,128)}, u32[]{:S(2)}) copy-start(s32[1,1,32]{2,1,0:T(1,128)} %param.14) | copy-start | bytes 388
  12.2 130.1 %copy-start.2 = (s32[1,1,32]{2,1,0:T(1,128)S(1)}, s32[1,1,32]{2,1,0:T(1,128)}, u32[]{:S(2)}) copy-start(s32[1,1,32]{2,1,0:T(1,128)} %param.13) | copy-start | bytes 388
  12.2 130.1 %all-to-all-start = ((bf16[16,256,1024]{2,1,0:T(8,128)(2,1)}), bf16[16,256,1024]{2,1,0:T(8,128)(2,1)}, u32[]{:S(2)}, u32[]{:S(2)}) async-start(bf16[16,256,1024]{2,1,0:T(8,128)(2,1)} %stack.4), calls=%async_computation | async-start | bytes 16777216 | tf_op jit(solution)/shard_map/all_to_all | solution.py:48
  20.1 379.2 %reduce-scatter.3.cloned.1.call-start = ((), (), s32[]{:S(2)}) async-start(), calls=%async_computation.4 | async-start | bytes 9437184 | tf_op jit(solution)/shard_map/reduce_scatter | solution.py:63
  277.1 0.7 copy-start.4
  277.1 26.6 %copy-start.3 = (s32[256]{0:T(256)S(1)}, s32[256]{0:T(256)}, u32[]{:S(2)}) copy-start(s32[256]{0:T(256)} %param.17) | copy-start | bytes 3076
  277.1 122.2 %copy-start = (f32[256,1024]{1,0:T(8,128)S(1)}, f32[256,1024]{1,0:T(8,128)}, u32[]{:S(2)}) copy-start(f32[256,1024]{1,0:T(8,128)} %param.16) | copy-start | bytes 3145732
  405.2 126.6 %all-to-all-start.1 = ((bf16[16,256,1024]{2,1,0:T(8,128)(2,1)}), bf16[16,256,1024]{2,1,0:T(8,128)(2,1)}, u32[]{:S(2)}, u32[]{:S(2)}) async-start(bf16[16,256,1024]{2,1,0:T(8,128)(2,1)} %stack.5), calls=%async_computation.2 | async-start | bytes 16777216 | tf_op jit(solution)/shard_map/all_to_all | solution.py:48
  410.9 375.1 %reduce-scatter.5.cloned.1.call-start = ((), (), s32[]{:S(2)}) async-start(), calls=%async_computation.5 | async-start | bytes 9437184 | tf_op jit(solution)/shard_map/reduce_scatter | solution.py:63
Sparse Core Ops, SparseCore 0:
  277.3 121.9 reduce-scatter.2
  666.6 119.3 reduce-scatter.4
